TPU v7x, 32 devices: a whole 2x2x4 slice. The times are simulated.
32 devices in a mesh: dp: 2 (over x), expert: 16 (over z, y, core).
Axes of the slice: x: 2, y: 2, z: 4, core: 2. Of those that a mesh axis runs over, the one named last changes fastest.
Arguments:
- out_grad: bfloat16 [4096, 1040], P(('dp', 'expert')), may hold values from -8 to 8
- routes: int32 [4096, 1], P(('dp', 'expert')), may hold values from 0 to 15; in each aligned block of 128 rows (0 to 127, 128 to 255, ...) at most 12 rows name the same one
- pre_act: bfloat16 [6144, 3072], P(('dp', 'expert')), may hold values from -6 to 6
- out_weight: bfloat16 [16, 3072, 1040], P('expert', 'dp'), may hold values from -0.109375 to 0.109375
- row_factor: float32 [16, 3072], P('expert', 'dp'), may hold values from 1 to 100
- col_factor: float32 [16, 1040], P('expert'), may hold values from 1 to 100
Outputs:
- hidden_grad: bfloat16 [4096, 3072], P(('dp', 'expert'))
- new_weight: bfloat16 [16, 3072, 1040], P('expert', 'dp')
- new_row: float32 [16, 3072], P('expert', 'dp')
- new_col: float32 [16, 1040], P('expert')
Inputs may be any that keep to these rules, and one draw needn't show every extreme that they name: `routes`: in the rows of one device no expert is named by more than 12 rows.
All inputs are finite; a program needn't handle non-finite values.
Results may differ from a plain program's by a relative error of at most 0.0025.
Values may be sent and summed in bfloat16 or wider, within the bound.
A program may use at most 64 MiB of HBM per device.

v0:
```python
import functools
import jax
import jax.numpy as jnp
import numpy as np
from jax import lax
from jax.experimental import pallas as pl
from jax.experimental.pallas import tpu as pltpu
from jax.sharding import PartitionSpec as P

MESH = pl.DeviceIdType.MESH
F32, BF16 = jnp.float32, jnp.bfloat16


def up128(n):
    return -(-n // 128) * 128


def dot(a, b, ca=1, cb=0):
    return lax.dot_general(a, b, (((ca,), (cb,)), ((), ())), preferred_element_type=F32)


def onehot(hit):
    return jnp.where(hit, 1.0, 0.0).astype(BF16)


def kernel(cfg, og, rrow, pre, w, rf, cf, qn, qt,
           hid, neww, newrow, newcol,
           dy_out, dy_all, dyn, pre_all, wv, grad, snd, ret, colst, place, colacc, cspad, cscol,
           loc, dy_s, dy_r, fw_s, fw_r, pre_s, pre_r, rt_s, rt_r, st_s, st_r):
    n_dp, n_e, slot, groups, chunk, deep = cfg
    d, tok = og.shape
    ff = wv.shape[1]
    r = pre.shape[0]
    packed = slot > 8
    half, dp_off, h0 = ff // 2, up128(d), d // 2 // 128 * 128
    rest = d - 2 * h0
    g = n_e // groups
    i, e = lax.axis_index("dp"), lax.axis_index("expert")
    total = n_dp * n_e
    flat = i * n_e + e
    others = [lax.rem(i + o, n_dp) for o in range(1, n_dp)]

    barrier = pltpu.get_barrier_semaphore()

    def greet(k, _):
        t = lax.rem(flat + k, total)
        ti = lax.div(t, n_e)
        pl.semaphore_signal(barrier, inc=1, device_id=(ti, t - ti * n_e), device_id_type=MESH)
        return 0

    lax.fori_loop(1, total, greet, 0)

    get_w = pltpu.make_async_copy(w.at[0], wv, loc.at[0])
    cols = lambda t: pl.ds(pl.multiple_of(t * ff, 128), ff)
    get_pre = pltpu.make_async_copy(pre.at[:, cols(i)], pre_all.at[i], loc.at[1])
    get_w.start()
    get_pre.start()

    named = jnp.broadcast_to(rrow[...].astype(F32), (tok, tok))
    same = named == named.T
    at_row = lax.broadcasted_iota(jnp.int32, (tok, tok), 0)
    at_col = lax.broadcasted_iota(jnp.int32, (tok, tok), 1)
    order = jnp.sum(jnp.where(same & (at_row < at_col), 1.0, 0.0), axis=0, keepdims=True)
    base = rrow[...].astype(F32) * 8.0 + order
    rows = lax.broadcasted_iota(jnp.int32, (n_e * 8, tok), 0).astype(F32)
    place[0] = onehot(rows == jnp.where(order < 8.0, base, -1.0))
    dy_out[:, :, 0:d] = dot(place[0], og[...], 1, 1).reshape(n_e, 8, d).astype(BF16)
    if packed:
        place[1] = onehot(rows == jnp.where(order >= 8.0, base - 8.0, -1.0))
        place[2] = onehot(rows == jnp.where(order >= 8.0, base - 4.0, -1.0))
        tail = dot(place[1], og[0:h0, :], 1, 1) + dot(place[2], og[h0:2 * h0, :], 1, 1)
        dy_out[:, :, dp_off:dp_off + h0] = tail.reshape(n_e, 8, h0).astype(BF16)
        if rest:
            more = dot(place[1], og[2 * h0:d, :], 1, 1)
            dy_out[:, :, d:d + rest] = more.reshape(n_e, 8, rest).astype(BF16)

    side = n_e // 2
    near = lax.div(e, side)
    far = 1 - near

    def over(which, k):
        return which * side + lax.rem(e + k, side)

    def send_dy(t):
        return pltpu.make_async_remote_copy(
            src_ref=dy_out.at[t], dst_ref=dy_all.at[i, e], send_sem=dy_s.at[t],
            recv_sem=dy_r.at[e], device_id=(i, t), device_id_type=MESH)

    def send_pre(t):
        return pltpu.make_async_remote_copy(
            src_ref=pre.at[:, cols(t)], dst_ref=pre_all.at[i], send_sem=pre_s.at[t],
            recv_sem=pre_r.at[i], device_id=(t, e), device_id_type=MESH)

    def send_fw(t, q):
        part = pl.ds(q * g, g)
        return pltpu.make_async_remote_copy(
            src_ref=dy_all.at[i, part], dst_ref=dy_all.at[i, part], send_sem=fw_s.at[t, q],
            recv_sem=fw_r.at[i, q], device_id=(t, e), device_id_type=MESH)

    def send_ret(t, j):
        return pltpu.make_async_remote_copy(
            src_ref=snd.at[t, j], dst_ref=ret.at[i, e], send_sem=rt_s.at[t, j],
            recv_sem=rt_r.at[i, e], device_id=(t, j), device_id_type=MESH)

    def send_st(t):
        return pltpu.make_async_remote_copy(
            src_ref=colst.at[i], dst_ref=colst.at[i], send_sem=st_s.at[t],
            recv_sem=st_r.at[i], device_id=(t, e), device_id_type=MESH)

    def loop(n, act):
        def step(k, _):
            act(k)
            return 0
        lax.fori_loop(0, n, step, 0)

    def all_peers(act):
        loop(side, lambda k: act(over(far, k)))
        loop(side - 1, lambda k: act(over(near, k + 1)))

    pl.semaphore_wait(barrier, total - 1)
    for t in others:
        send_pre(t).start()
    all_peers(lambda t: send_dy(t).start())
    own = pltpu.make_async_copy(dy_out.at[e], dy_all.at[i, e], dy_r.at[e])
    own.start()

    colacc[...] = jnp.zeros_like(colacc)

    def receive(which):
        for k in range(groups // 2):
            q = which * (groups // 2) + k
            for m in range(g):
                j = q * g + m
                pltpu.make_async_copy(dy_out.at[0], dy_all.at[i, j], dy_r.at[j]).wait()
            for t in others:
                send_fw(t, q).start()

    def flat_rows(x):
        return x.astype(F32).reshape(x.shape[0] * 8, x.shape[2]).astype(BF16)

    def back(t, first, count):
        n = count * slot
        part = pl.ds(first, count)
        where = pl.ds(first * slot if isinstance(first, int) else pl.multiple_of(first * slot, 16), n)
        dy = dot(qn[0, 0:n, 0:count * 8], flat_rows(dy_all[t, part, :, 0:d]))
        if packed:
            q_lo, q_hi = qn[1, 0:n, 0:count * 8], qn[2, 0:n, 0:count * 8]
            tail = flat_rows(dy_all[t, part, :, dp_off:dp_off + h0])
            pieces = [dot(q_lo, tail), dot(q_hi, tail)]
            if rest:
                ends = dot(q_lo, flat_rows(dy_all[t, part, :, 2 * h0:dp_off]))
                pieces.append(ends[:, d - 2 * h0:d - 2 * h0 + rest])
            dy = dy + jnp.concatenate(pieces, axis=1)
        dy = dy.astype(BF16)
        dyn[t, where, :] = dy
        tail = None
        for c in range(2 if packed else 1):
            wide = half if packed else ff
            span = slice(c * wide, c * wide + wide)
            bk = dot(dy, wv[:, span])
            keep = pre_all[t, where, span].astype(F32) > 0.0
            bk = jnp.where(keep, bk, 0.0).astype(BF16)
            snd[t, part, :, span] = dot(qt[0, 0:count * 8, 0:n], bk).reshape(count, 8, wide).astype(BF16)
            if packed:
                more = dot(qt[1 + c, 0:count * 8, 0:n], bk)
                tail = more if tail is None else tail + more
        if packed:
            snd[t, part, :, ff:ff + half] = tail.reshape(count, 8, half).astype(BF16)

    receive(far)
    get_w.wait()
    get_pre.wait()
    back(i, far * side, side)
    loop(side, lambda k: send_ret(i, over(far, k)).start())
    receive(near)
    back(i, near * side, side)
    loop(side - 1, lambda k: send_ret(i, over(near, k + 1)).start())
    own_ret = pltpu.make_async_copy(snd.at[i, e], ret.at[i, e], rt_r.at[i, e])
    own_ret.start()

    def send_side(t, which):
        loop(side, lambda k: send_ret(t, over(which, k)).start())

    for t in others:
        pltpu.make_async_copy(pre_all.at[i], pre_all.at[t], pre_r.at[t]).wait()
        for which in (far, near):
            for k in range(groups // 2):
                q = which * (groups // 2) + k
                part = pl.ds(q * g, g)
                pltpu.make_async_copy(dy_all.at[i, part], dy_all.at[t, part], fw_r.at[t, q]).wait()
            back(t, which * side, side)
            if which is far:
                send_side(t, far)

    def gradient(c):
        span = pl.ds(pl.multiple_of(c * chunk, 128), chunk)
        acc = None
        for t in range(n_dp):
            part = dot(dyn[t], jnp.maximum(pre_all[t, :, span], 0), 0, 0)
            acc = part if acc is None else acc + part
        grad[:, span] = acc
        sq = acc * acc
        rn = 0.8 * rf[0:1, span] + 0.2 * (jnp.sum(sq, axis=0, keepdims=True) / d + 1e-30)
        newrow[0:1, span] = rn
        for k, x in enumerate((sq, sq * (1.0 / rn))):
            folded = x[:, 0:128]
            for b in range(1, chunk // 128):
                folded = folded + x[:, b * 128:b * 128 + 128]
            colacc[k, 0:d, :] += folded

    loop(ff // chunk, gradient)
    blocks = [(b, min(b + 128, d)) for b in range(0, d, 128)]
    for k in range(2):
        for lo, hi in blocks:
            sums = jnp.sum(colacc[k, lo:lo + 128, :].T, axis=0, keepdims=True)
            colst[i, k:k + 1, lo:hi] = sums[:, 0:hi - lo]
    for t in others:
        send_st(t).start()
        send_side(t, near)
    for t in others:
        pltpu.make_async_copy(colst.at[i], colst.at[t], st_r.at[t]).wait()
    col, weighted = jnp.zeros((1, d), F32), jnp.zeros((1, d), F32)
    for t in range(n_dp):
        col = col + colst[t, 0:1, :]
        weighted = weighted + colst[t, 1:2, :]
    full = ff * n_dp
    cn = 0.8 * cf[...] + 0.2 * (col / full + 1e-30)
    newcol[...] = cn
    spread = jnp.sqrt(jnp.sum(weighted / cn, axis=1, keepdims=True) / (full * d))
    cspad[...] = jnp.zeros_like(cspad)
    cspad[0:1, 0:d] = lax.rsqrt(cn) / jnp.maximum(1.0, spread / 0.01)
    for lo, hi in blocks:
        cscol[lo:lo + 128, :] = jnp.broadcast_to(cspad[0:1, lo:lo + 128], (128, 128)).T

    def apply(c):
        span = pl.ds(pl.multiple_of(c * deep, 16), deep)
        update = grad[span, :] * lax.rsqrt(newrow[...]) * cscol[span, 0:1]
        neww[0, span, :] = (wv[span, :].astype(F32) - update).astype(BF16)

    loop(d // deep, apply)

    for t in [i] + others:
        loop(n_e, lambda j: pltpu.make_async_copy(
            snd.at[0, 0], ret.at[t, j], rt_r.at[t, j]).wait())
        for c in range(2 if packed else 1):
            wide = half if packed else ff
            got = dot(place[0], flat_rows(ret[t, :, :, c * wide:c * wide + wide]), 0, 0)
            if packed:
                got = got + dot(place[1 + c], flat_rows(ret[t, :, :, ff:ff + half]), 0, 0)
            hid[:, pl.ds(pl.multiple_of(t * ff + c * wide, 128), wide)] = got.astype(BF16)

    all_peers(lambda t: send_dy(t).wait_send())
    all_peers(lambda t: send_ret(i, t).wait_send())
    for t in others:
        send_pre(t).wait_send()
        for q in range(groups):
            send_fw(t, q).wait_send()
        loop(n_e, lambda k: send_ret(t, k).wait_send())
        send_st(t).wait_send()


def flush(a, b, c, d, ao, bo, co, do, sem):
    pairs = ((b, bo), (a, ao), (c, co), (d, do))
    copies = [pltpu.make_async_copy(x, y, sem.at[k]) for k, (x, y) in enumerate(pairs)]
    for copy in copies:
        copy.start()
    for copy in copies:
        copy.wait()


def shards(out_grad, routes, pre_act, out_weight, row_factor, col_factor):
    n_dp, n_e = lax.axis_size("dp"), lax.axis_size("expert")
    tok, d = out_grad.shape
    r = pre_act.shape[0]
    ff = out_weight.shape[1]
    slot = r // n_e
    packed = slot > 8
    assert slot <= 12
    kinds = 3 if packed else 1
    groups = 4
    chunk = next(c for c in (384, 256, 128) if ff % c == 0)
    deep = max(c for c in range(16, 257, 16) if d % c == 0)
    wide_d = up128(d) + d // 2 // 128 * 128 if packed else d
    assert not packed or 2 * d - d // 256 * 256 <= up128(d)
    wide_f = ff + ff // 2 if packed else ff
    row = np.arange(r)
    src, s = row // slot, row % slot
    q = np.zeros((kinds, r, n_e * 8), np.float32)
    low = s < 8
    q[0, row[low], (src * 8 + s)[low]] = 1
    if packed:
        q[1, row[~low], (src * 8 + s - 8)[~low]] = 1
        q[2, row[~low], (src * 8 + s - 4)[~low]] = 1
    qn = jnp.asarray(q, BF16)
    qt = jnp.asarray(q.transpose(0, 2, 1), BF16)
    vm = pl.BlockSpec(memory_space=pltpu.VMEM)
    hbm = pl.BlockSpec(memory_space=pl.ANY)
    dma = pltpu.SemaphoreType.DMA
    out = pltpu.VMEM
    hid, neww, newrow, newcol = pl.pallas_call(
        functools.partial(kernel, (n_dp, n_e, slot, groups, chunk, deep)),
        out_shape=(out((tok, ff * n_dp), BF16), out((1, d, ff), BF16),
                   out((1, ff), F32), out((1, d), F32)),
        in_specs=[vm, vm, hbm, hbm, vm, vm, vm, vm],
        out_specs=(vm, vm, vm, vm),
        scratch_shapes=[
            pltpu.VMEM((n_e, 8, wide_d), BF16),
            pltpu.VMEM((n_dp, n_e, 8, wide_d), BF16),
            pltpu.VMEM((n_dp, r, d), BF16),
            pltpu.VMEM((n_dp, r, ff), BF16),
            pltpu.VMEM((d, ff), BF16),
            pltpu.VMEM((d, ff), F32),
            pltpu.VMEM((n_dp, n_e, 8, wide_f), BF16),
            pltpu.VMEM((n_dp, n_e, 8, wide_f), BF16),
            pltpu.VMEM((n_dp, 2, d), F32),
            pltpu.VMEM((kinds, n_e * 8, tok), BF16),
            pltpu.VMEM((2, up128(d), 128), F32),
            pltpu.VMEM((1, up128(d)), F32),
            pltpu.VMEM((up128(d), 128), F32),
            dma((2,)), dma((n_e,)), dma((n_e,)),
            dma((n_dp, groups)), dma((n_dp, groups)), dma((n_dp,)), dma((n_dp,)),
            dma((n_dp, n_e)), dma((n_dp, n_e)), dma((n_dp,)), dma((n_dp,)),
        ],
        compiler_params=pltpu.CompilerParams(
            collective_id=0, has_side_effects=True, vmem_limit_bytes=59 * 1024 * 1024),
    )(out_grad.T, routes.reshape(1, tok), pre_act, jnp.swapaxes(out_weight, 1, 2), row_factor,
      col_factor, qn, qt)
    held = (hid, neww, newrow, newcol)
    hid, neww, newrow, newcol = pl.pallas_call(
        flush,
        out_shape=tuple(jax.ShapeDtypeStruct(x.shape, x.dtype) for x in held),
        in_specs=[vm] * 4,
        out_specs=[hbm] * 4,
        scratch_shapes=[dma((4,))],
        compiler_params=pltpu.CompilerParams(vmem_limit_bytes=1024 * 1024),
    )(*held)
    return hid, jnp.swapaxes(neww, 1, 2), newrow, newcol


def solution(mesh):
    placed = (
        P(("dp", "expert"), None),
        P(("dp", "expert"), None),
        P(("dp", "expert"), None),
        P("expert", "dp", None),
        P("expert", "dp"),
        P("expert", None),
    )
    return jax.shard_map(
        shards,
        mesh=mesh,
        in_specs=placed,
        out_specs=(
            P(("dp", "expert"), None),
            P("expert", "dp", None),
            P("expert", "dp"),
            P("expert", None),
        ),
        check_vma=False,
    )
```

profile of v0, /device:TPU:0, one launch (start us, length us, event | category | flops | bytes accessed | tf_op | source)
XLA Modules:
  0.0 53.5 jit_solution(7569420222657812416)
XLA Ops:
  0.6 50.9 %shard_map.111 = (bf16[128,3072]{1,0:T(8,128)(2,1)S(1)}, bf16[1,1040,1536]{2,1,0:T(8,128)(2,1)S(1)}, f32[1,1536]{1,0:T(1,128)S(1)}, f32[1,1040]{1,0:T(1,128)S(1)}) custom-call(bf16[1040,128]{1,0:T(8,128)(2,1)} %bitcast.5, s32[1,128]{1,0:T(1,128)} %bitcast.6, bf16[192,3072]{1,0:T(8,128)(2,1)} %pre.1, bf16[1,1040,1536]{2,1,0:T(8,128)(2,1)} %bitcast.4, ...), custom_call_target="tpu_custom_call" | custom-call | tf_op jit(solution)/shard_map/pallas_call | solution.py:300
  51.5 2.0 %shard_map.112 = (bf16[128,3072]{1,0:T(8,128)(2,1)}, bf16[1,1040,1536]{2,1,0:T(8,128)(2,1)}, f32[1,1536]{1,0:T(1,128)}, f32[1,1040]{1,0:T(1,128)}) custom-call(bf16[128,3072]{1,0:T(8,128)(2,1)S(1)} %get-tuple-element.12.a, bf16[1,1040,1536]{2,1,0:T(8,128)(2,1)S(1)} %get-tuple-element.13.b, f32[1,1536]{1,0:T(1,128)S(1)} %get-tuple-element.14.c, ...), custom_call_target="tpu_custom_call" | custom-call | tf_op jit(solution)/shard_map/pallas_call | solution.py:329
where the time goes:
time: 53.6 us; the launch traced here: 53.5 us
  Pallas kernels  52.8 us (99%)
  between operations  0.64 us (1%)
    pallas_call x1, Pallas kernels, shards(): pl.pallas_call(functools.partial(kernel, (n_dp, n_e, slot, groups, chunk,...  50.9 us
    pallas_call x1, Pallas kernels, shards(): pl.pallas_call(flush, out_shape=tuple((jax.ShapeDtypeStruct(x.shape, x.dt...  1.97 us

commit v1 on v0

v1 whole, which is shorter than its diff:
```python
import functools
import jax
import jax.numpy as jnp
from jax import lax
from jax.experimental import pallas as pl
from jax.experimental.pallas import tpu as pltpu
from jax.sharding import PartitionSpec as P

MESH = pl.DeviceIdType.MESH
F32, BF16 = jnp.float32, jnp.bfloat16


def up128(n):
    return -(-n // 128) * 128


def dot(a, b, ca=1, cb=0):
    return lax.dot_general(a, b, (((ca,), (cb,)), ((), ())), preferred_element_type=F32)


def onehot(hit):
    return jnp.where(hit, 1.0, 0.0).astype(BF16)


def kernel(cfg, og_h, rrow_h, pre, w, rf_h, cf_h,
           hid, neww, newrow, newcol,
           og, rrow, rf, cf, qn, qt,
           dy_out, dy_all, dyn, pre_all, wv, grad, snd, ret, colst, place, colacc, cspad, cscol,
           loc, flood, dy_s, dy_r, fw_s, fw_r, pre_s, pre_r, rt_s, rt_r, st_s, st_r):
    n_dp, n_e, slot, chunk, deep = cfg
    d, tok = og.shape
    ff = wv.shape[1]
    packed = slot > 8
    half, dp_off, h0 = ff // 2, up128(d), d // 2 // 128 * 128
    rest = d - 2 * h0
    bits = n_e.bit_length() - 1
    g = n_e // 4
    n = g * slot
    i, e = lax.axis_index("dp"), lax.axis_index("expert")
    others = [(o, lax.rem(i + o, n_dp)) for o in range(1, n_dp)]

    def flip(x, b):
        return x + (1 - 2 * lax.rem(lax.div(x, 1 << b), 2)) * (1 << b)

    def loop(count, act):
        def step(k, _):
            act(k)
            return 0
        lax.fori_loop(0, count, step, 0)

    barrier = pltpu.get_barrier_semaphore()
    for _, t in others:
        pl.semaphore_signal(barrier, inc=1, device_id=(t, e), device_id_type=MESH)
    for b in range(bits):
        pl.semaphore_signal(barrier, inc=1, device_id=(i, flip(e, b)), device_id_type=MESH)

    cols = lambda t: pl.ds(pl.multiple_of(t * ff, 128), ff)
    loads = [pltpu.make_async_copy(x, y, loc.at[k]) for k, (x, y) in enumerate((
        (rrow_h, rrow), (og_h, og), (w.at[0], wv), (pre.at[:, cols(i)], pre_all.at[i]), (rf_h, rf),
        (cf_h, cf)))]
    for load in loads:
        load.start()

    def tables(q, rows, cells, axis):
        for k in range(q.shape[0]):
            row = lax.broadcasted_iota(jnp.int32, (rows, cells), axis)
            cell = lax.broadcasted_iota(jnp.int32, (rows, cells), 1 - axis)
            at = cell & 7
            wants = slot * (cell >> 3) + at + (0, 8, 4)[k]
            held = (at < min(slot, 8), at < slot - 8, at >= 4)[k]
            q[k] = onehot((row == wants) & held)

    tables(qn, n, g * 8, 0)
    tables(qt, g * 8, n, 1)

    loads[0].wait()
    named = jnp.broadcast_to(rrow[...].astype(F32), (tok, tok))
    same = named == named.T
    at_row = lax.broadcasted_iota(jnp.int32, (tok, tok), 0)
    at_col = lax.broadcasted_iota(jnp.int32, (tok, tok), 1)
    order = jnp.sum(jnp.where(same & (at_row < at_col), 1.0, 0.0), axis=0, keepdims=True)
    base = rrow[...].astype(F32) * 8.0 + order
    rows = lax.broadcasted_iota(jnp.int32, (n_e * 8, tok), 0).astype(F32)
    place[0] = onehot(rows == jnp.where(order < 8.0, base, -1.0))
    if packed:
        place[1] = onehot(rows == jnp.where(order >= 8.0, base - 8.0, -1.0))
        place[2] = onehot(rows == jnp.where(order >= 8.0, base - 4.0, -1.0))
    loads[1].wait()
    dy_out[:, :, 0:d] = dot(place[0], og[...], 1, 1).reshape(n_e, 8, d).astype(BF16)
    if packed:
        tail = dot(place[1], og[0:h0, :], 1, 1) + dot(place[2], og[h0:2 * h0, :], 1, 1)
        dy_out[:, :, dp_off:dp_off + h0] = tail.reshape(n_e, 8, h0).astype(BF16)
        if rest:
            more = dot(place[1], og[2 * h0:d, :], 1, 1)
            dy_out[:, :, d:d + rest] = more.reshape(n_e, 8, rest).astype(BF16)

    quarter = lax.div(e, g)
    order_k = (2, 3, 1, 0)
    group = {0: quarter, 1: flip(quarter, 0), 2: flip(quarter, 1), 3: flip(flip(quarter, 0), 1)}

    def members(k, act):
        if k:
            loop(g, lambda m: act(group[k] * g + m))
        else:
            loop(g - 1, lambda m: act(quarter * g + lax.rem(e + 1 + m, g)))

    def send_dy(k, t):
        return pltpu.make_async_remote_copy(
            src_ref=dy_out.at[t], dst_ref=dy_all.at[i, e], send_sem=dy_s.at[0],
            recv_sem=dy_r.at[k], device_id=(i, t), device_id_type=MESH)

    def send_pre(o, t):
        return pltpu.make_async_remote_copy(
            src_ref=pre.at[:, cols(t)], dst_ref=pre_all.at[i], send_sem=pre_s.at[o - 1],
            recv_sem=pre_r.at[n_dp - o - 1], device_id=(t, e), device_id_type=MESH)

    def send_fw(o, t, k):
        part = pl.ds(group[k] * g, g)
        return pltpu.make_async_remote_copy(
            src_ref=dy_all.at[i, part], dst_ref=dy_all.at[i, part], send_sem=fw_s.at[o - 1],
            recv_sem=fw_r.at[n_dp - o - 1, k], device_id=(t, e), device_id_type=MESH)

    def send_ret(o, t, j):
        return pltpu.make_async_remote_copy(
            src_ref=snd.at[t, j], dst_ref=ret.at[i, e], send_sem=rt_s.at[o],
            recv_sem=rt_r.at[lax.rem(n_dp - o, n_dp)], device_id=(t, j), device_id_type=MESH)

    def send_st(o, t):
        return pltpu.make_async_remote_copy(
            src_ref=colst.at[i], dst_ref=colst.at[i], send_sem=st_s.at[o - 1],
            recv_sem=st_r.at[n_dp - o - 1], device_id=(t, e), device_id_type=MESH)

    def meet(b):
        pl.semaphore_signal(flood.at[b], inc=1, device_id=(i, flip(e, b)), device_id_type=MESH)
        pl.semaphore_wait(flood.at[b], 1)

    with jax.named_scope("bar"):
        pl.semaphore_wait(barrier, bits + n_dp - 1)
    for o, t in others:
        send_pre(o, t).start()
    with jax.named_scope("flood"):
        for b in range(bits - 2):
            meet(b)
    members(2, lambda t: send_dy(2, t).start())
    with jax.named_scope("flood2"):
        meet(bits - 2)
    for k in (3, 1, 0):
        members(k, lambda t: send_dy(k, t).start())
    own = pltpu.make_async_copy(dy_out.at[e], dy_all.at[i, e], dy_r.at[0])
    own.start()

    colacc[...] = jnp.zeros_like(colacc)

    def flat_rows(x):
        return x.astype(F32).reshape(x.shape[0] * 8, x.shape[2]).astype(BF16)

    def back(t, k):
        part = pl.ds(group[k] * g, g)
        where = pl.ds(pl.multiple_of(group[k] * n, 16), n)
        dy = dot(qn[0], flat_rows(dy_all[t, part, :, 0:d]))
        if packed:
            q_lo, q_hi = qn[1], qn[2]
            tail = flat_rows(dy_all[t, part, :, dp_off:dp_off + h0])
            pieces = [dot(q_lo, tail), dot(q_hi, tail)]
            if rest:
                ends = dot(q_lo, flat_rows(dy_all[t, part, :, 2 * h0:dp_off]))
                pieces.append(ends[:, d - 2 * h0:d - 2 * h0 + rest])
            dy = dy + jnp.concatenate(pieces, axis=1)
        dy = dy.astype(BF16)
        dyn[t, where, :] = dy
        tail = None
        for c in range(2 if packed else 1):
            wide = half if packed else ff
            span = slice(c * wide, c * wide + wide)
            bk = dot(dy, wv[:, span])
            keep = pre_all[t, where, span].astype(F32) > 0.0
            bk = jnp.where(keep, bk, 0.0).astype(BF16)
            snd[t, part, :, span] = dot(qt[0], bk).reshape(g, 8, wide).astype(BF16)
            if packed:
                more = dot(qt[1 + c], bk)
                tail = more if tail is None else tail + more
        if packed:
            snd[t, part, :, ff:ff + half] = tail.reshape(g, 8, half).astype(BF16)

    for k in order_k:
        part = pl.ds(group[k] * g, g)
        with jax.named_scope("recv%d" % k):
            pltpu.make_async_copy(dy_all.at[0, part], dy_all.at[i, part], dy_r.at[k]).wait()
        for o, t in others:
            send_fw(o, t, k).start()
        if k == order_k[0]:
            with jax.named_scope("waitw"):
                loads[2].wait()
                loads[3].wait()
        with jax.named_scope("back%d" % k):
            back(i, k)
        members(k, lambda j: send_ret(0, i, j).start())
    own_ret = pltpu.make_async_copy(snd.at[i, e], ret.at[i, e], rt_r.at[0])
    own_ret.start()

    for o, t in others:
        with jax.named_scope("waitpre"):
            pltpu.make_async_copy(pre_all.at[i], pre_all.at[t], pre_r.at[o - 1]).wait()
        for k in order_k:
            part = pl.ds(group[k] * g, g)
            with jax.named_scope("waitfw%d" % k):
                pltpu.make_async_copy(dy_all.at[i, part], dy_all.at[t, part], fw_r.at[o - 1, k]).wait()
            with jax.named_scope("backx%d" % k):
                back(t, k)
            loop(g, lambda m: send_ret(o, t, group[k] * g + m).start())

    loads[4].wait()
    loads[5].wait()

    def gradient(c):
        span = pl.ds(pl.multiple_of(c * chunk, 128), chunk)
        acc = None
        for t in range(n_dp):
            part = dot(dyn[t], jnp.maximum(pre_all[t, :, span], 0), 0, 0)
            acc = part if acc is None else acc + part
        grad[:, span] = acc
        sq = acc * acc
        rn = 0.8 * rf[0:1, span] + 0.2 * (jnp.sum(sq, axis=0, keepdims=True) / d + 1e-30)
        newrow[0:1, span] = rn
        for k, x in enumerate((sq, sq * (1.0 / rn))):
            folded = x[:, 0:128]
            for b in range(1, chunk // 128):
                folded = folded + x[:, b * 128:b * 128 + 128]
            colacc[k, 0:d, :] += folded

    with jax.named_scope("grad"):
        loop(ff // chunk, gradient)
    blocks = [(b, min(b + 128, d)) for b in range(0, d, 128)]
    for k in range(2):
        for lo, hi in blocks:
            sums = jnp.sum(colacc[k, lo:lo + 128, :].T, axis=0, keepdims=True)
            colst[i, k:k + 1, lo:hi] = sums[:, 0:hi - lo]
    for o, t in others:
        send_st(o, t).start()

    def deliver(o, t):
        with jax.named_scope("waitret%d" % o):
            pltpu.make_async_copy(snd.at[0], ret.at[t], rt_r.at[o]).wait()
        with jax.named_scope("hid%d" % o):
            for c in range(2 if packed else 1):
                wide = half if packed else ff
                got = dot(place[0], flat_rows(ret[t, :, :, c * wide:c * wide + wide]), 0, 0)
                if packed:
                    got = got + dot(place[1 + c], flat_rows(ret[t, :, :, ff:ff + half]), 0, 0)
                hid[:, pl.ds(pl.multiple_of(t * ff + c * wide, 128), wide)] = got.astype(BF16)

    deliver(0, i)
    with jax.named_scope("waitst"):
        for o, t in others:
            pltpu.make_async_copy(colst.at[i], colst.at[t], st_r.at[o - 1]).wait()
    col, weighted = jnp.zeros((1, d), F32), jnp.zeros((1, d), F32)
    for t in range(n_dp):
        col = col + colst[t, 0:1, :]
        weighted = weighted + colst[t, 1:2, :]
    full = ff * n_dp
    cn = 0.8 * cf[...] + 0.2 * (col / full + 1e-30)
    newcol[...] = cn
    spread = jnp.sqrt(jnp.sum(weighted / cn, axis=1, keepdims=True) / (full * d))
    cspad[...] = jnp.zeros_like(cspad)
    cspad[0:1, 0:d] = lax.rsqrt(cn) / jnp.maximum(1.0, spread / 0.01)
    for lo, hi in blocks:
        cscol[lo:lo + 128, :] = jnp.broadcast_to(cspad[0:1, lo:lo + 128], (128, 128)).T

    def apply(c):
        span = pl.ds(pl.multiple_of(c * deep, 16), deep)
        update = grad[span, :] * lax.rsqrt(newrow[...]) * cscol[span, 0:1]
        neww[0, span, :] = (wv[span, :].astype(F32) - update).astype(BF16)

    with jax.named_scope("apply"):
        loop(d // deep, apply)

    for o, t in others:
        deliver(o, t)

    def sent(src, sem):
        pltpu.make_async_copy(src, src, sem).wait()

    with jax.named_scope("sent"):
        sent(dy_out.at[0:n_e - 1], dy_s.at[0])
        sent(snd.at[0, 0:n_e - 1], rt_s.at[0])
        for o, t in others:
            sent(pre_all.at[0], pre_s.at[o - 1])
            sent(dy_all.at[0], fw_s.at[o - 1])
            sent(snd.at[0], rt_s.at[o])
            sent(colst.at[0], st_s.at[o - 1])


def flush(a, b, c, d, ao, bo, co, do, sem):
    pairs = ((b, bo), (a, ao), (c, co), (d, do))
    copies = [pltpu.make_async_copy(x, y, sem.at[k]) for k, (x, y) in enumerate(pairs)]
    for copy in copies:
        copy.start()
    for copy in copies:
        copy.wait()


def shards(out_grad, routes, pre_act, out_weight, row_factor, col_factor):
    n_dp, n_e = lax.axis_size("dp"), lax.axis_size("expert")
    tok, d = out_grad.shape
    r = pre_act.shape[0]
    ff = out_weight.shape[1]
    slot = r // n_e
    packed = slot > 8
    assert slot <= 12
    kinds = 3 if packed else 1
    assert n_e >= 4 and n_e & (n_e - 1) == 0
    g = n_e // 4
    chunk = next(c for c in (384, 256, 128) if ff % c == 0)
    deep = max(c for c in range(16, 257, 16) if d % c == 0)
    wide_d = up128(d) + d // 2 // 128 * 128 if packed else d
    assert not packed or 2 * d - d // 256 * 256 <= up128(d)
    wide_f = ff + ff // 2 if packed else ff
    vm = pl.BlockSpec(memory_space=pltpu.VMEM)
    hbm = pl.BlockSpec(memory_space=pl.ANY)
    dma = pltpu.SemaphoreType.DMA
    out = pltpu.VMEM
    hid, neww, newrow, newcol = pl.pallas_call(
        functools.partial(kernel, (n_dp, n_e, slot, chunk, deep)),
        out_shape=(out((tok, ff * n_dp), BF16), out((1, d, ff), BF16),
                   out((1, ff), F32), out((1, d), F32)),
        in_specs=[hbm] * 6,
        out_specs=(vm, vm, vm, vm),
        scratch_shapes=[
            pltpu.VMEM((d, tok), BF16),
            pltpu.VMEM((1, tok), jnp.int32),
            pltpu.VMEM((1, ff), F32),
            pltpu.VMEM((1, d), F32),
            pltpu.VMEM((kinds, g * slot, g * 8), BF16),
            pltpu.VMEM((kinds, g * 8, g * slot), BF16),
            pltpu.VMEM((n_e, 8, wide_d), BF16),
            pltpu.VMEM((n_dp, n_e, 8, wide_d), BF16),
            pltpu.VMEM((n_dp, r, d), BF16),
            pltpu.VMEM((n_dp, r, ff), BF16),
            pltpu.VMEM((d, ff), BF16),
            pltpu.VMEM((d, ff), F32),
            pltpu.VMEM((n_dp, n_e, 8, wide_f), BF16),
            pltpu.VMEM((n_dp, n_e, 8, wide_f), BF16),
            pltpu.VMEM((n_dp, 2, d), F32),
            pltpu.VMEM((kinds, n_e * 8, tok), BF16),
            pltpu.VMEM((2, up128(d), 128), F32),
            pltpu.VMEM((1, up128(d)), F32),
            pltpu.VMEM((up128(d), 128), F32),
            dma((6,)), pltpu.SemaphoreType.REGULAR((n_e.bit_length() - 2,)), dma((1,)), dma((4,)),
            dma((n_dp - 1,)), dma((n_dp - 1, 4)), dma((n_dp - 1,)), dma((n_dp - 1,)),
            dma((n_dp,)), dma((n_dp,)), dma((n_dp - 1,)), dma((n_dp - 1,)),
        ],
        compiler_params=pltpu.CompilerParams(
            collective_id=0, has_side_effects=True, vmem_limit_bytes=59 * 1024 * 1024),
    )(out_grad.T, routes.reshape(1, tok), pre_act, jnp.swapaxes(out_weight, 1, 2), row_factor,
      col_factor)
    held = (hid, neww, newrow, newcol)
    hid, neww, newrow, newcol = pl.pallas_call(
        flush,
        out_shape=tuple(jax.ShapeDtypeStruct(x.shape, x.dtype) for x in held),
        in_specs=[vm] * 4,
        out_specs=[hbm] * 4,
        scratch_shapes=[dma((4,))],
        compiler_params=pltpu.CompilerParams(vmem_limit_bytes=1024 * 1024),
    )(*held)
    return hid, jnp.swapaxes(neww, 1, 2), newrow, newcol


def solution(mesh):
    placed = (
        P(("dp", "expert"), None),
        P(("dp", "expert"), None),
        P(("dp", "expert"), None),
        P("expert", "dp", None),
        P("expert", "dp"),
        P("expert", None),
    )
    return jax.shard_map(
        shards,
        mesh=mesh,
        in_specs=placed,
        out_specs=(
            P(("dp", "expert"), None),
            P("expert", "dp", None),
            P("expert", "dp"),
            P("expert", None),
        ),
        check_vma=False,
    )
```

time: 53.6 us -> 47.5 us (0.89)
  Pallas kernels: 52.8 us -> 46.7 us
    pallas_call x1, Pallas kernels: 50.9 us -> 44.7 us  [shards(): pl.pallas_call(functools.partial(kernel, (n_dp, n_e, slot, chunk, deep)),...]
where the time goes in v1:
time: 47.5 us; the launch traced here: 47.3 us
  Pallas kernels  46.7 us (98%)
  between operations  0.64 us (1%)
    pallas_call x1, Pallas kernels, shards(): pl.pallas_call(functools.partial(kernel, (n_dp, n_e, slot, chunk, deep)),...  44.7 us
    pallas_call x1, Pallas kernels, shards(): pl.pallas_call(flush, out_shape=tuple((jax.ShapeDtypeStruct(x.shape, x.dt...  1.97 us

profile of v1, /device:TPU:0, one launch (start us, length us, event | category | flops | bytes accessed | tf_op | source)
XLA Modules:
  0.0 47.3 jit_solution(6738170035676682444)
XLA Ops:
  0.6 44.7 %shard_map.93 = (bf16[128,3072]{1,0:T(8,128)(2,1)S(1)}, bf16[1,1040,1536]{2,1,0:T(8,128)(2,1)S(1)}, f32[1,1536]{1,0:T(1,128)S(1)}, f32[1,1040]{1,0:T(1,128)S(1)}) custom-call(bf16[1040,128]{1,0:T(8,128)(2,1)} %bitcast.5, s32[1,128]{1,0:T(1,128)} %bitcast.6, bf16[192,3072]{1,0:T(8,128)(2,1)} %pre.1, bf16[1,1040,1536]{2,1,0:T(8,128)(2,1)} %bitcast.4, ...), custom_call_target="tpu_custom_call" | custom-call | tf_op jit(solution)/shard_map/pallas_call | solution.py:322
  45.4 2.0 %shard_map.94 = (bf16[128,3072]{1,0:T(8,128)(2,1)}, bf16[1,1040,1536]{2,1,0:T(8,128)(2,1)}, f32[1,1536]{1,0:T(1,128)}, f32[1,1040]{1,0:T(1,128)}) custom-call(bf16[128,3072]{1,0:T(8,128)(2,1)S(1)} %get-tuple-element.12.a, bf16[1,1040,1536]{2,1,0:T(8,128)(2,1)S(1)} %get-tuple-element.13.b, f32[1,1536]{1,0:T(1,128)S(1)} %get-tuple-element.14.c, ...), custom_call_target="tpu_custom_call" | custom-call | tf_op jit(solution)/shard_map/pallas_call | solution.py:357

commit v2 on v1

--- a/solution.py
+++ b/solution.py
@@ -22,10 +22,14 @@
     return jnp.where(hit, 1.0, 0.0).astype(BF16)
 
 
+def flat_rows(x):
+    return x.astype(F32).reshape(x.shape[0] * 8, x.shape[2]).astype(BF16)
+
+
 def kernel(cfg, og_h, rrow_h, pre, w, rf_h, cf_h,
-           hid, neww, newrow, newcol,
+           ret, place, neww, newrow, newcol,
            og, rrow, rf, cf, qn, qt,
-           dy_out, dy_all, dyn, pre_all, wv, grad, snd, ret, colst, place, colacc, cspad, cscol,
+           dy_out, dy_all, dyn, pre_all, wv, grad, snd, colst, colacc, cspad, cscol,
            loc, flood, dy_s, dy_r, fw_s, fw_r, pre_s, pre_r, rt_s, rt_r, st_s, st_r):
     n_dp, n_e, slot, chunk, deep = cfg
     d, tok = og.shape
@@ -95,7 +99,6 @@
             dy_out[:, :, d:d + rest] = more.reshape(n_e, 8, rest).astype(BF16)
 
     quarter = lax.div(e, g)
-    order_k = (2, 3, 1, 0)
     group = {0: quarter, 1: flip(quarter, 0), 2: flip(quarter, 1), 3: flip(flip(quarter, 0), 1)}
 
     def members(k, act):
@@ -109,10 +112,14 @@
             src_ref=dy_out.at[t], dst_ref=dy_all.at[i, e], send_sem=dy_s.at[0],
             recv_sem=dy_r.at[k], device_id=(i, t), device_id_type=MESH)
 
-    def send_pre(o, t):
+    def rows_of(k):
+        return pl.ds(pl.multiple_of(group[k] * n, 16), n)
+
+    def send_pre(o, t, k):
         return pltpu.make_async_remote_copy(
-            src_ref=pre.at[:, cols(t)], dst_ref=pre_all.at[i], send_sem=pre_s.at[o - 1],
-            recv_sem=pre_r.at[n_dp - o - 1], device_id=(t, e), device_id_type=MESH)
+            src_ref=pre.at[rows_of(k), cols(t)], dst_ref=pre_all.at[i, rows_of(k)],
+            send_sem=pre_s.at[o - 1], recv_sem=pre_r.at[n_dp - o - 1, k], device_id=(t, e),
+            device_id_type=MESH)
 
     def send_fw(o, t, k):
         part = pl.ds(group[k] * g, g)
@@ -136,12 +143,16 @@
 
     with jax.named_scope("bar"):
         pl.semaphore_wait(barrier, bits + n_dp - 1)
-    for o, t in others:
-        send_pre(o, t).start()
+    for k in (2, 3, 1):
+        for o, t in others:
+            send_pre(o, t, k).start()
+    across = flip(e, bits - 1)
+    send_dy(2, across).start()
     with jax.named_scope("flood"):
         for b in range(bits - 2):
             meet(b)
-    members(2, lambda t: send_dy(2, t).start())
+            first = lax.div(flip(across, b), 1 << b) * (1 << b)
+            loop(1 << b, lambda m: send_dy(2, first + m).start())
     with jax.named_scope("flood2"):
         meet(bits - 2)
     for k in (3, 1, 0):
@@ -151,12 +162,9 @@
 
     colacc[...] = jnp.zeros_like(colacc)
 
-    def flat_rows(x):
-        return x.astype(F32).reshape(x.shape[0] * 8, x.shape[2]).astype(BF16)
-
     def back(t, k):
         part = pl.ds(group[k] * g, g)
-        where = pl.ds(pl.multiple_of(group[k] * n, 16), n)
+        where = rows_of(k)
         dy = dot(qn[0], flat_rows(dy_all[t, part, :, 0:d]))
         if packed:
             q_lo, q_hi = qn[1], qn[2]
@@ -182,32 +190,68 @@
         if packed:
             snd[t, part, :, ff:ff + half] = tail.reshape(g, 8, half).astype(BF16)
 
-    for k in order_k:
+    def arrive(k):
         part = pl.ds(group[k] * g, g)
         with jax.named_scope("recv%d" % k):
             pltpu.make_async_copy(dy_all.at[0, part], dy_all.at[i, part], dy_r.at[k]).wait()
+
+    def forward(k):
         for o, t in others:
             send_fw(o, t, k).start()
-        if k == order_k[0]:
-            with jax.named_scope("waitw"):
-                loads[2].wait()
-                loads[3].wait()
+
+    def near(k):
         with jax.named_scope("back%d" % k):
             back(i, k)
         members(k, lambda j: send_ret(0, i, j).start())
+
+    def await_cross(k):
+        part = pl.ds(group[k] * g, g)
+        for o, t in others:
+            with jax.named_scope("waitpre%d" % k):
+                pltpu.make_async_copy(
+                    pre_all.at[i, rows_of(k)], pre_all.at[t, rows_of(k)], pre_r.at[o - 1, k]).wait()
+            with jax.named_scope("waitfw%d" % k):
+                pltpu.make_async_copy(dy_all.at[i, part], dy_all.at[t, part], fw_r.at[o - 1, k]).wait()
+
+    def back_cross(k):
+        for _, t in others:
+            with jax.named_scope("backx%d" % k):
+                back(t, k)
+
+    def cross(k):
+        await_cross(k)
+        back_cross(k)
+
+    def send_cross(k):
+        for o, t in others:
+            loop(g, lambda m: send_ret(o, t, group[k] * g + m).start())
+
+    arrive(2)
+    forward(2)
+    loads[2].wait()
+    loads[3].wait()
+    near(2)
+    arrive(3)
+    forward(3)
+    for o, t in others:
+        send_pre(o, t, 0).start()
+    near(3)
+    arrive(1)
+    forward(1)
+    near(1)
+    arrive(0)
+    forward(0)
+    near(0)
     own_ret = pltpu.make_async_copy(snd.at[i, e], ret.at[i, e], rt_r.at[0])
     own_ret.start()
-
-    for o, t in others:
-        with jax.named_scope("waitpre"):
-            pltpu.make_async_copy(pre_all.at[i], pre_all.at[t], pre_r.at[o - 1]).wait()
-        for k in order_k:
-            part = pl.ds(group[k] * g, g)
-            with jax.named_scope("waitfw%d" % k):
-                pltpu.make_async_copy(dy_all.at[i, part], dy_all.at[t, part], fw_r.at[o - 1, k]).wait()
-            with jax.named_scope("backx%d" % k):
-                back(t, k)
-            loop(g, lambda m: send_ret(o, t, group[k] * g + m).start())
+    cross(2)
+    cross(3)
+    cross(1)
+    send_cross(2)
+    send_cross(3)
+    await_cross(0)
+    send_cross(1)
+    back_cross(0)
 
     loads[4].wait()
     loads[5].wait()
@@ -237,19 +281,8 @@
             colst[i, k:k + 1, lo:hi] = sums[:, 0:hi - lo]
     for o, t in others:
         send_st(o, t).start()
-
-    def deliver(o, t):
-        with jax.named_scope("waitret%d" % o):
-            pltpu.make_async_copy(snd.at[0], ret.at[t], rt_r.at[o]).wait()
-        with jax.named_scope("hid%d" % o):
-            for c in range(2 if packed else 1):
-                wide = half if packed else ff
-                got = dot(place[0], flat_rows(ret[t, :, :, c * wide:c * wide + wide]), 0, 0)
-                if packed:
-                    got = got + dot(place[1 + c], flat_rows(ret[t, :, :, ff:ff + half]), 0, 0)
-                hid[:, pl.ds(pl.multiple_of(t * ff + c * wide, 128), wide)] = got.astype(BF16)
-
-    deliver(0, i)
+    send_cross(0)
+
     with jax.named_scope("waitst"):
         for o, t in others:
             pltpu.make_async_copy(colst.at[i], colst.at[t], st_r.at[o - 1]).wait()
@@ -274,8 +307,9 @@
     with jax.named_scope("apply"):
         loop(d // deep, apply)
 
-    for o, t in others:
-        deliver(o, t)
+    for o, t in [(0, i)] + others:
+        with jax.named_scope("waitret%d" % o):
+            pltpu.make_async_copy(snd.at[0], ret.at[t], rt_r.at[o]).wait()
 
     def sent(src, sem):
         pltpu.make_async_copy(src, src, sem).wait()
@@ -290,11 +324,22 @@
             sent(colst.at[0], st_s.at[o - 1])
 
 
-def flush(a, b, c, d, ao, bo, co, do, sem):
-    pairs = ((b, bo), (a, ao), (c, co), (d, do))
-    copies = [pltpu.make_async_copy(x, y, sem.at[k]) for k, (x, y) in enumerate(pairs)]
+def finish(packed, ff, ret, place, neww, newrow, newcol, hid_o, neww_o, newrow_o, newcol_o, hid, sem):
+    copies = [pltpu.make_async_copy(x, y, sem.at[k]) for k, (x, y) in enumerate((
+        (neww, neww_o), (newrow, newrow_o), (newcol, newcol_o)))]
     for copy in copies:
         copy.start()
+    half = ff // 2
+    wide = half if packed else ff
+    for t in range(ret.shape[0]):
+        for c in range(2 if packed else 1):
+            got = dot(place[0], flat_rows(ret[t, :, :, c * wide:c * wide + wide]), 0, 0)
+            if packed:
+                got = got + dot(place[1 + c], flat_rows(ret[t, :, :, ff:ff + half]), 0, 0)
+            hid[:, t * ff + c * wide:t * ff + c * wide + wide] = got.astype(BF16)
+        span = slice(t * ff, t * ff + ff)
+        copies.append(pltpu.make_async_copy(hid.at[:, span], hid_o.at[:, span], sem.at[3 + t]))
+        copies[-1].start()
     for copy in copies:
         copy.wait()
 
@@ -319,12 +364,12 @@
     hbm = pl.BlockSpec(memory_space=pl.ANY)
     dma = pltpu.SemaphoreType.DMA
     out = pltpu.VMEM
-    hid, neww, newrow, newcol = pl.pallas_call(
+    held = pl.pallas_call(
         functools.partial(kernel, (n_dp, n_e, slot, chunk, deep)),
-        out_shape=(out((tok, ff * n_dp), BF16), out((1, d, ff), BF16),
-                   out((1, ff), F32), out((1, d), F32)),
+        out_shape=(out((n_dp, n_e, 8, wide_f), BF16), out((kinds, n_e * 8, tok), BF16),
+                   out((1, d, ff), BF16), out((1, ff), F32), out((1, d), F32)),
         in_specs=[hbm] * 6,
-        out_specs=(vm, vm, vm, vm),
+        out_specs=(vm,) * 5,
         scratch_shapes=[
             pltpu.VMEM((d, tok), BF16),
             pltpu.VMEM((1, tok), jnp.int32),
@@ -339,28 +384,26 @@
             pltpu.VMEM((d, ff), BF16),
             pltpu.VMEM((d, ff), F32),
             pltpu.VMEM((n_dp, n_e, 8, wide_f), BF16),
-            pltpu.VMEM((n_dp, n_e, 8, wide_f), BF16),
             pltpu.VMEM((n_dp, 2, d), F32),
-            pltpu.VMEM((kinds, n_e * 8, tok), BF16),
             pltpu.VMEM((2, up128(d), 128), F32),
             pltpu.VMEM((1, up128(d)), F32),
             pltpu.VMEM((up128(d), 128), F32),
-            dma((6,)), pltpu.SemaphoreType.REGULAR((n_e.bit_length() - 2,)), dma((1,)), dma((4,)),
-            dma((n_dp - 1,)), dma((n_dp - 1, 4)), dma((n_dp - 1,)), dma((n_dp - 1,)),
+            dma((6,)), pltpu.SemaphoreType.REGULAR((n_e.bit_length() - 1,)), dma((1,)), dma((4,)),
+            dma((n_dp - 1,)), dma((n_dp - 1, 4)), dma((n_dp - 1,)), dma((n_dp - 1, 4)),
             dma((n_dp,)), dma((n_dp,)), dma((n_dp - 1,)), dma((n_dp - 1,)),
         ],
         compiler_params=pltpu.CompilerParams(
             collective_id=0, has_side_effects=True, vmem_limit_bytes=59 * 1024 * 1024),
     )(out_grad.T, routes.reshape(1, tok), pre_act, jnp.swapaxes(out_weight, 1, 2), row_factor,
       col_factor)
-    held = (hid, neww, newrow, newcol)
     hid, neww, newrow, newcol = pl.pallas_call(
-        flush,
-        out_shape=tuple(jax.ShapeDtypeStruct(x.shape, x.dtype) for x in held),
-        in_specs=[vm] * 4,
+        functools.partial(finish, packed, ff),
+        out_shape=tuple(jax.ShapeDtypeStruct(*x) for x in (
+            ((tok, ff * n_dp), BF16), ((1, d, ff), BF16), ((1, ff), F32), ((1, d), F32))),
+        in_specs=[vm] * 5,
         out_specs=[hbm] * 4,
-        scratch_shapes=[dma((4,))],
-        compiler_params=pltpu.CompilerParams(vmem_limit_bytes=1024 * 1024),
+        scratch_shapes=[pltpu.VMEM((tok, ff * n_dp), BF16), dma((3 + n_dp,))],
+        compiler_params=pltpu.CompilerParams(vmem_limit_bytes=8 * 1024 * 1024),
     )(*held)
     return hid, jnp.swapaxes(neww, 1, 2), newrow, newcol
 

time: 47.5 us -> 45.8 us (0.964)
  the two profiles are of different devices: /device:TPU:0 before, /device:TPU:15 now
where the time goes in v2:
time: 45.8 us; the launch traced here: 45.6 us
  Pallas kernels  45 us (98%)
  between operations  0.64 us (1%)
    pallas_call x1, Pallas kernels, shards(): pl.pallas_call(functools.partial(kernel, (n_dp, n_e, slot, chunk, deep)),...  43 us
    pallas_call x1, Pallas kernels, shards(): pl.pallas_call(functools.partial(finish, packed, ff), out_shape=tuple((ja...  1.98 us

profile of v2, /device:TPU:15, one launch (start us, length us, event | category | flops | bytes accessed | tf_op | source)
XLA Modules:
  0.0 45.6 jit_solution(1477691582663706769)
XLA Ops:
  0.6 43.0 %shard_map.93 = (bf16[2,16,8,2304]{3,2,1,0:T(8,128)(2,1)S(1)}, bf16[3,128,128]{2,1,0:T(8,128)(2,1)S(1)}, bf16[1,1040,1536]{2,1,0:T(8,128)(2,1)S(1)}, f32[1,1536]{1,0:T(1,128)S(1)}, f32[1,1040]{1,0:T(1,128)S(1)}) custom-call(bf16[1040,128]{1,0:T(8,128)(2,1)} %bitcast.5, s32[1,128]{1,0:T(1,128)} %bitcast.6, bf16[192,3072]{1,0:T(8,128)(2,1)} %pre.1, ...), custom_call_target="tpu_custom_call" | custom-call | tf_op jit(solution)/shard_map/pallas_call | solution.py:367
  43.6 2.0 %shard_map.94 = (bf16[128,3072]{1,0:T(8,128)(2,1)}, bf16[1,1040,1536]{2,1,0:T(8,128)(2,1)}, f32[1,1536]{1,0:T(1,128)}, f32[1,1040]{1,0:T(1,128)}) custom-call(bf16[2,16,8,2304]{3,2,1,0:T(8,128)(2,1)S(1)} %get-tuple-element.13.ret, bf16[3,128,128]{2,1,0:T(8,128)(2,1)S(1)} %get-tuple-element.14.place, bf16[1,1040,1536]{2,1,0:T(8,128)(2,1)S(1)} %get-tuple-element.15.neww, ...), custom_call_target="tpu_custom_call" | custom-call | tf_op jit(solution)/shard_map/pallas_call | solution.py:399

commit v3 on v2

--- a/solution.py
+++ b/solution.py
@@ -143,7 +143,7 @@
 
     with jax.named_scope("bar"):
         pl.semaphore_wait(barrier, bits + n_dp - 1)
-    for k in (2, 3, 1):
+    for k in (2, 3, 1, 0):
         for o, t in others:
             send_pre(o, t, k).start()
     across = flip(e, bits - 1)
@@ -233,8 +233,6 @@
     near(2)
     arrive(3)
     forward(3)
-    for o, t in others:
-        send_pre(o, t, 0).start()
     near(3)
     arrive(1)
     forward(1)

time: 45.8 us -> 44.4 us (0.969)
  the two profiles are of different devices: /device:TPU:15 before, /device:TPU:0 now
where the time goes in v3:
time: 44.4 us; the launch traced here: 44.1 us
  Pallas kernels  43.4 us (98%)
  between operations  0.64 us (1%)
    pallas_call x1, Pallas kernels, shards(): pl.pallas_call(functools.partial(kernel, (n_dp, n_e, slot, chunk, deep)),...  41.5 us
    pallas_call x1, Pallas kernels, shards(): pl.pallas_call(functools.partial(finish, packed, ff), out_shape=tuple((ja...  1.98 us

profile of v3, /device:TPU:0, one launch (start us, length us, event | category | flops | bytes accessed | tf_op | source)
XLA Modules:
  0.0 44.1 jit_solution(2272348579387818155)
XLA Ops:
  0.6 41.5 %shard_map.93 = (bf16[2,16,8,2304]{3,2,1,0:T(8,128)(2,1)S(1)}, bf16[3,128,128]{2,1,0:T(8,128)(2,1)S(1)}, bf16[1,1040,1536]{2,1,0:T(8,128)(2,1)S(1)}, f32[1,1536]{1,0:T(1,128)S(1)}, f32[1,1040]{1,0:T(1,128)S(1)}) custom-call(bf16[1040,128]{1,0:T(8,128)(2,1)} %bitcast.5, s32[1,128]{1,0:T(1,128)} %bitcast.6, bf16[192,3072]{1,0:T(8,128)(2,1)} %pre.1, ...), custom_call_target="tpu_custom_call" | custom-call | tf_op jit(solution)/shard_map/pallas_call | solution.py:365
  42.1 2.0 %shard_map.94 = (bf16[128,3072]{1,0:T(8,128)(2,1)}, bf16[1,1040,1536]{2,1,0:T(8,128)(2,1)}, f32[1,1536]{1,0:T(1,128)}, f32[1,1040]{1,0:T(1,128)}) custom-call(bf16[2,16,8,2304]{3,2,1,0:T(8,128)(2,1)S(1)} %get-tuple-element.13.ret, bf16[3,128,128]{2,1,0:T(8,128)(2,1)S(1)} %get-tuple-element.14.place, bf16[1,1040,1536]{2,1,0:T(8,128)(2,1)S(1)} %get-tuple-element.15.neww, ...), custom_call_target="tpu_custom_call" | custom-call | tf_op jit(solution)/shard_map/pallas_call | solution.py:397

commit v4 on v3

--- a/solution.py
+++ b/solution.py
@@ -28,7 +28,7 @@
 
 def kernel(cfg, og_h, rrow_h, pre, w, rf_h, cf_h,
            ret, place, neww, newrow, newcol,
-           og, rrow, rf, cf, qn, qt,
+           og, rrow, rf, cf, qn, qt, eye, ends,
            dy_out, dy_all, dyn, pre_all, wv, grad, snd, colst, colacc, cspad, cscol,
            loc, flood, dy_s, dy_r, fw_s, fw_r, pre_s, pre_r, rt_s, rt_r, st_s, st_r):
     n_dp, n_e, slot, chunk, deep = cfg
@@ -37,6 +37,7 @@
     packed = slot > 8
     half, dp_off, h0 = ff // 2, up128(d), d // 2 // 128 * 128
     rest = d - 2 * h0
+    main, last = d // 128 * 128, d % 128
     bits = n_e.bit_length() - 1
     g = n_e // 4
     n = g * slot
@@ -76,6 +77,9 @@
 
     tables(qn, n, g * 8, 0)
     tables(qt, g * 8, n, 1)
+    if last:
+        eye[...] = onehot(lax.broadcasted_iota(jnp.int32, (n, 128), 0)
+                          == lax.broadcasted_iota(jnp.int32, (n, 128), 1))
 
     loads[0].wait()
     named = jnp.broadcast_to(rrow[...].astype(F32), (tok, tok))
@@ -99,6 +103,8 @@
             dy_out[:, :, d:d + rest] = more.reshape(n_e, 8, rest).astype(BF16)
 
     quarter = lax.div(e, g)
+    inner = lax.rem(quarter + 1, 4) >= 2
+    outer = lax.rem(quarter + 1, 4) < 2
     group = {0: quarter, 1: flip(quarter, 0), 2: flip(quarter, 1), 3: flip(flip(quarter, 0), 1)}
 
     def members(k, act):
@@ -109,7 +115,7 @@
 
     def send_dy(k, t):
         return pltpu.make_async_remote_copy(
-            src_ref=dy_out.at[t], dst_ref=dy_all.at[i, e], send_sem=dy_s.at[0],
+            src_ref=dy_out.at[t], dst_ref=dy_all.at[e], send_sem=dy_s.at[0],
             recv_sem=dy_r.at[k], device_id=(i, t), device_id_type=MESH)
 
     def rows_of(k):
@@ -122,10 +128,10 @@
             device_id_type=MESH)
 
     def send_fw(o, t, k):
-        part = pl.ds(group[k] * g, g)
-        return pltpu.make_async_remote_copy(
-            src_ref=dy_all.at[i, part], dst_ref=dy_all.at[i, part], send_sem=fw_s.at[o - 1],
-            recv_sem=fw_r.at[n_dp - o - 1, k], device_id=(t, e), device_id_type=MESH)
+        refs = [dyn.at[i, rows_of(k), 0:main]] + ([ends.at[i, group[k]]] if last else [])
+        return [pltpu.make_async_remote_copy(
+            src_ref=x, dst_ref=x, send_sem=fw_s.at[o - 1, m], recv_sem=fw_r.at[n_dp - o - 1, k, m],
+            device_id=(t, e), device_id_type=MESH) for m, x in enumerate(refs)]
 
     def send_ret(o, t, j):
         return pltpu.make_async_remote_copy(
@@ -157,25 +163,31 @@
         meet(bits - 2)
     for k in (3, 1, 0):
         members(k, lambda t: send_dy(k, t).start())
-    own = pltpu.make_async_copy(dy_out.at[e], dy_all.at[i, e], dy_r.at[0])
+    own = pltpu.make_async_copy(dy_out.at[e], dy_all.at[e], dy_r.at[0])
     own.start()
 
     colacc[...] = jnp.zeros_like(colacc)
 
-    def back(t, k):
+    def unpack(k):
+        part = pl.ds(group[k] * g, g)
+        dy = dot(qn[0], flat_rows(dy_all[part, :, 0:d]))
+        if packed:
+            q_lo, q_hi = qn[1], qn[2]
+            tail = flat_rows(dy_all[part, :, dp_off:dp_off + h0])
+            pieces = [dot(q_lo, tail), dot(q_hi, tail)]
+            if rest:
+                more = dot(q_lo, flat_rows(dy_all[part, :, 2 * h0:dp_off]))
+                pieces.append(more[:, d - 2 * h0:d - 2 * h0 + rest])
+            dy = dy + jnp.concatenate(pieces, axis=1)
+        dy = dy.astype(BF16)
+        dyn[i, rows_of(k), :] = dy
+        if last:
+            ends[i, group[k]] = dot(dy[:, main:d], eye[...], 0, 0).astype(BF16)
+        return dy
+
+    def back(t, k, dy):
         part = pl.ds(group[k] * g, g)
         where = rows_of(k)
-        dy = dot(qn[0], flat_rows(dy_all[t, part, :, 0:d]))
-        if packed:
-            q_lo, q_hi = qn[1], qn[2]
-            tail = flat_rows(dy_all[t, part, :, dp_off:dp_off + h0])
-            pieces = [dot(q_lo, tail), dot(q_hi, tail)]
-            if rest:
-                ends = dot(q_lo, flat_rows(dy_all[t, part, :, 2 * h0:dp_off]))
-                pieces.append(ends[:, d - 2 * h0:d - 2 * h0 + rest])
-            dy = dy + jnp.concatenate(pieces, axis=1)
-        dy = dy.astype(BF16)
-        dyn[t, where, :] = dy
         tail = None
         for c in range(2 if packed else 1):
             wide = half if packed else ff
@@ -193,73 +205,90 @@
     def arrive(k):
         part = pl.ds(group[k] * g, g)
         with jax.named_scope("recv%d" % k):
-            pltpu.make_async_copy(dy_all.at[0, part], dy_all.at[i, part], dy_r.at[k]).wait()
+            pltpu.make_async_copy(dy_out.at[part], dy_all.at[part], dy_r.at[k]).wait()
 
     def forward(k):
         for o, t in others:
-            send_fw(o, t, k).start()
+            for copy in send_fw(o, t, k):
+                copy.start()
 
     def near(k):
         with jax.named_scope("back%d" % k):
-            back(i, k)
+            back(i, k, unpack(k))
         members(k, lambda j: send_ret(0, i, j).start())
 
     def await_cross(k):
-        part = pl.ds(group[k] * g, g)
         for o, t in others:
             with jax.named_scope("waitpre%d" % k):
                 pltpu.make_async_copy(
                     pre_all.at[i, rows_of(k)], pre_all.at[t, rows_of(k)], pre_r.at[o - 1, k]).wait()
             with jax.named_scope("waitfw%d" % k):
-                pltpu.make_async_copy(dy_all.at[i, part], dy_all.at[t, part], fw_r.at[o - 1, k]).wait()
+                rows = dyn.at[t, rows_of(k), 0:main]
+                pltpu.make_async_copy(rows, rows, fw_r.at[o - 1, k, 0]).wait()
+                if last:
+                    tile = ends.at[t, group[k]]
+                    pltpu.make_async_copy(tile, tile, fw_r.at[o - 1, k, 1]).wait()
+                    dyn[t, rows_of(k), main:d] = dot(eye[...], ends[t, group[k]], 1, 1).astype(BF16)
 
     def back_cross(k):
         for _, t in others:
             with jax.named_scope("backx%d" % k):
-                back(t, k)
+                back(t, k, dyn[t, rows_of(k), :])
 
     def cross(k):
         await_cross(k)
         back_cross(k)
 
-    def send_cross(k):
-        for o, t in others:
-            loop(g, lambda m: send_ret(o, t, group[k] * g + m).start())
+    def send_cross(k, first=0, count=g):
+        for o, t in others:
+            loop(count, lambda m: send_ret(o, t, group[k] * g + first + m).start())
 
     arrive(2)
-    forward(2)
     loads[2].wait()
     loads[3].wait()
     near(2)
+    forward(2)
     arrive(3)
+    near(3)
     forward(3)
-    near(3)
     arrive(1)
+    near(1)
     forward(1)
-    near(1)
     arrive(0)
+    near(0)
     forward(0)
-    near(0)
     own_ret = pltpu.make_async_copy(snd.at[i, e], ret.at[i, e], rt_r.at[0])
     own_ret.start()
+    def gradient_own(c):
+        span = pl.ds(pl.multiple_of(c * chunk, 128), chunk)
+        grad[:, span] = dot(dyn[i], jnp.maximum(pre_all[i, :, span], 0), 0, 0)
+
+    with jax.named_scope("gradown"):
+        loop(ff // chunk, gradient_own)
     cross(2)
     cross(3)
     cross(1)
     send_cross(2)
     send_cross(3)
     await_cross(0)
-    send_cross(1)
+    @pl.when(inner)
+    def _():
+        send_cross(1)
+
     back_cross(0)
+    @pl.when(inner)
+    def _():
+        send_cross(0, 0, g // 2)
+
 
     loads[4].wait()
     loads[5].wait()
 
     def gradient(c):
         span = pl.ds(pl.multiple_of(c * chunk, 128), chunk)
-        acc = None
-        for t in range(n_dp):
-            part = dot(dyn[t], jnp.maximum(pre_all[t, :, span], 0), 0, 0)
-            acc = part if acc is None else acc + part
+        acc = grad[:, span]
+        for _, t in others:
+            acc = acc + dot(dyn[t], jnp.maximum(pre_all[t, :, span], 0), 0, 0)
         grad[:, span] = acc
         sq = acc * acc
         rn = 0.8 * rf[0:1, span] + 0.2 * (jnp.sum(sq, axis=0, keepdims=True) / d + 1e-30)
@@ -279,7 +308,18 @@
             colst[i, k:k + 1, lo:hi] = sums[:, 0:hi - lo]
     for o, t in others:
         send_st(o, t).start()
-    send_cross(0)
+    @pl.when(outer)
+    def _():
+        send_cross(1)
+
+    @pl.when(inner)
+    def _():
+        send_cross(0, g // 2, g // 2)
+
+    @pl.when(jnp.logical_not(inner))
+    def _():
+        send_cross(0)
+
 
     with jax.named_scope("waitst"):
         for o, t in others:
@@ -317,7 +357,9 @@
         sent(snd.at[0, 0:n_e - 1], rt_s.at[0])
         for o, t in others:
             sent(pre_all.at[0], pre_s.at[o - 1])
-            sent(dy_all.at[0], fw_s.at[o - 1])
+            sent(dyn.at[0, :, 0:main], fw_s.at[o - 1, 0])
+            if last:
+                sent(ends.at[0], fw_s.at[o - 1, 1])
             sent(snd.at[0], rt_s.at[o])
             sent(colst.at[0], st_s.at[o - 1])
 
@@ -353,6 +395,7 @@
     kinds = 3 if packed else 1
     assert n_e >= 4 and n_e & (n_e - 1) == 0
     g = n_e // 4
+    assert g * slot <= 128
     chunk = next(c for c in (384, 256, 128) if ff % c == 0)
     deep = max(c for c in range(16, 257, 16) if d % c == 0)
     wide_d = up128(d) + d // 2 // 128 * 128 if packed else d
@@ -375,8 +418,10 @@
             pltpu.VMEM((1, d), F32),
             pltpu.VMEM((kinds, g * slot, g * 8), BF16),
             pltpu.VMEM((kinds, g * 8, g * slot), BF16),
+            pltpu.VMEM((g * slot, 128), BF16),
+            pltpu.VMEM((n_dp, 4, max(d % 128, 1), 128), BF16),
             pltpu.VMEM((n_e, 8, wide_d), BF16),
-            pltpu.VMEM((n_dp, n_e, 8, wide_d), BF16),
+            pltpu.VMEM((n_e, 8, wide_d), BF16),
             pltpu.VMEM((n_dp, r, d), BF16),
             pltpu.VMEM((n_dp, r, ff), BF16),
             pltpu.VMEM((d, ff), BF16),
@@ -387,7 +432,7 @@
             pltpu.VMEM((1, up128(d)), F32),
             pltpu.VMEM((up128(d), 128), F32),
             dma((6,)), pltpu.SemaphoreType.REGULAR((n_e.bit_length() - 1,)), dma((1,)), dma((4,)),
-            dma((n_dp - 1,)), dma((n_dp - 1, 4)), dma((n_dp - 1,)), dma((n_dp - 1, 4)),
+            dma((n_dp - 1, 2)), dma((n_dp - 1, 4, 2)), dma((n_dp - 1,)), dma((n_dp - 1, 4)),
             dma((n_dp,)), dma((n_dp,)), dma((n_dp - 1,)), dma((n_dp - 1,)),
         ],
         compiler_params=pltpu.CompilerParams(

time: 44.4 us -> 44 us (level)
  no operation moved by 1% of the time
where the time goes in v4:
time: 44 us; the launch traced here: 43.8 us
  Pallas kernels  43.1 us (98%)
  between operations  0.64 us (1%)
    pallas_call x1, Pallas kernels, shards(): pl.pallas_call(functools.partial(kernel, (n_dp, n_e, slot, chunk, deep)),...  41.2 us
    pallas_call x1, Pallas kernels, shards(): pl.pallas_call(functools.partial(finish, packed, ff), out_shape=tuple((ja...  1.98 us

profile of v4, /device:TPU:0, one launch (start us, length us, event | category | flops | bytes accessed | tf_op | source)
XLA Modules:
  0.0 43.8 jit_solution(13415863516245287315)
XLA Ops:
  0.6 41.2 %shard_map.93 = (bf16[2,16,8,2304]{3,2,1,0:T(8,128)(2,1)S(1)}, bf16[3,128,128]{2,1,0:T(8,128)(2,1)S(1)}, bf16[1,1040,1536]{2,1,0:T(8,128)(2,1)S(1)}, f32[1,1536]{1,0:T(1,128)S(1)}, f32[1,1040]{1,0:T(1,128)S(1)}) custom-call(bf16[1040,128]{1,0:T(8,128)(2,1)} %bitcast.5, s32[1,128]{1,0:T(1,128)} %bitcast.6, bf16[192,3072]{1,0:T(8,128)(2,1)} %pre.1, ...), custom_call_target="tpu_custom_call" | custom-call | tf_op jit(solution)/shard_map/pallas_call | solution.py:408
  41.8 2.0 %shard_map.94 = (bf16[128,3072]{1,0:T(8,128)(2,1)}, bf16[1,1040,1536]{2,1,0:T(8,128)(2,1)}, f32[1,1536]{1,0:T(1,128)}, f32[1,1040]{1,0:T(1,128)}) custom-call(bf16[2,16,8,2304]{3,2,1,0:T(8,128)(2,1)S(1)} %get-tuple-element.13.ret, bf16[3,128,128]{2,1,0:T(8,128)(2,1)S(1)} %get-tuple-element.14.place, bf16[1,1040,1536]{2,1,0:T(8,128)(2,1)S(1)} %get-tuple-element.15.neww, ...), custom_call_target="tpu_custom_call" | custom-call | tf_op jit(solution)/shard_map/pallas_call | solution.py:442

commit v5 on v4

--- a/solution.py
+++ b/solution.py
@@ -121,10 +121,10 @@
     def rows_of(k):
         return pl.ds(pl.multiple_of(group[k] * n, 16), n)
 
-    def send_pre(o, t, k):
+    def send_pre(o, t):
         return pltpu.make_async_remote_copy(
-            src_ref=pre.at[rows_of(k), cols(t)], dst_ref=pre_all.at[i, rows_of(k)],
-            send_sem=pre_s.at[o - 1], recv_sem=pre_r.at[n_dp - o - 1, k], device_id=(t, e),
+            src_ref=pre.at[:, cols(t)], dst_ref=pre_all.at[i],
+            send_sem=pre_s.at[o - 1], recv_sem=pre_r.at[n_dp - o - 1], device_id=(t, e),
             device_id_type=MESH)
 
     def send_fw(o, t, k):
@@ -149,9 +149,8 @@
 
     with jax.named_scope("bar"):
         pl.semaphore_wait(barrier, bits + n_dp - 1)
-    for k in (2, 3, 1, 0):
-        for o, t in others:
-            send_pre(o, t, k).start()
+    for o, t in others:
+        send_pre(o, t).start()
     across = flip(e, bits - 1)
     send_dy(2, across).start()
     with jax.named_scope("flood"):
@@ -219,9 +218,6 @@
 
     def await_cross(k):
         for o, t in others:
-            with jax.named_scope("waitpre%d" % k):
-                pltpu.make_async_copy(
-                    pre_all.at[i, rows_of(k)], pre_all.at[t, rows_of(k)], pre_r.at[o - 1, k]).wait()
             with jax.named_scope("waitfw%d" % k):
                 rows = dyn.at[t, rows_of(k), 0:main]
                 pltpu.make_async_copy(rows, rows, fw_r.at[o - 1, k, 0]).wait()
@@ -265,6 +261,8 @@
 
     with jax.named_scope("gradown"):
         loop(ff // chunk, gradient_own)
+    for o, t in others:
+        pltpu.make_async_copy(pre_all.at[i], pre_all.at[t], pre_r.at[o - 1]).wait()
     cross(2)
     cross(3)
     cross(1)
@@ -432,7 +430,7 @@
             pltpu.VMEM((1, up128(d)), F32),
             pltpu.VMEM((up128(d), 128), F32),
             dma((6,)), pltpu.SemaphoreType.REGULAR((n_e.bit_length() - 1,)), dma((1,)), dma((4,)),
-            dma((n_dp - 1, 2)), dma((n_dp - 1, 4, 2)), dma((n_dp - 1,)), dma((n_dp - 1, 4)),
+            dma((n_dp - 1, 2)), dma((n_dp - 1, 4, 2)), dma((n_dp - 1,)), dma((n_dp - 1,)),
             dma((n_dp,)), dma((n_dp,)), dma((n_dp - 1,)), dma((n_dp - 1,)),
         ],
         compiler_params=pltpu.CompilerParams(

time: 44 us -> 44 us (level)
  no operation moved by 1% of the time
where the time goes in v5:
time: 44 us; the launch traced here: 43.8 us
  Pallas kernels  43.1 us (98%)
  between operations  0.64 us (1%)
    pallas_call x1, Pallas kernels, shards(): pl.pallas_call(functools.partial(kernel, (n_dp, n_e, slot, chunk, deep)),...  41.1 us
    pallas_call x1, Pallas kernels, shards(): pl.pallas_call(functools.partial(finish, packed, ff), out_shape=tuple((ja...  1.98 us

profile of v5, /device:TPU:0, one launch (start us, length us, event | category | flops | bytes accessed | tf_op | source)
XLA Modules:
  0.0 43.8 jit_solution(8185533154101338099)
XLA Ops:
  0.6 41.1 %shard_map.93 = (bf16[2,16,8,2304]{3,2,1,0:T(8,128)(2,1)S(1)}, bf16[3,128,128]{2,1,0:T(8,128)(2,1)S(1)}, bf16[1,1040,1536]{2,1,0:T(8,128)(2,1)S(1)}, f32[1,1536]{1,0:T(1,128)S(1)}, f32[1,1040]{1,0:T(1,128)S(1)}) custom-call(bf16[1040,128]{1,0:T(8,128)(2,1)} %bitcast.5, s32[1,128]{1,0:T(1,128)} %bitcast.6, bf16[192,3072]{1,0:T(8,128)(2,1)} %pre.1, ...), custom_call_target="tpu_custom_call" | custom-call | tf_op jit(solution)/shard_map/pallas_call | solution.py:406
  41.8 2.0 %shard_map.94 = (bf16[128,3072]{1,0:T(8,128)(2,1)}, bf16[1,1040,1536]{2,1,0:T(8,128)(2,1)}, f32[1,1536]{1,0:T(1,128)}, f32[1,1040]{1,0:T(1,128)}) custom-call(bf16[2,16,8,2304]{3,2,1,0:T(8,128)(2,1)S(1)} %get-tuple-element.13.ret, bf16[3,128,128]{2,1,0:T(8,128)(2,1)S(1)} %get-tuple-element.14.place, bf16[1,1040,1536]{2,1,0:T(8,128)(2,1)S(1)} %get-tuple-element.15.neww, ...), custom_call_target="tpu_custom_call" | custom-call | tf_op jit(solution)/shard_map/pallas_call | solution.py:440

commit v6 on v5

--- a/solution.py
+++ b/solution.py
@@ -255,15 +255,15 @@
     forward(0)
     own_ret = pltpu.make_async_copy(snd.at[i, e], ret.at[i, e], rt_r.at[0])
     own_ret.start()
+    for o, t in others:
+        pltpu.make_async_copy(pre_all.at[i], pre_all.at[t], pre_r.at[o - 1]).wait()
+    cross(2)
     def gradient_own(c):
         span = pl.ds(pl.multiple_of(c * chunk, 128), chunk)
         grad[:, span] = dot(dyn[i], jnp.maximum(pre_all[i, :, span], 0), 0, 0)
 
     with jax.named_scope("gradown"):
         loop(ff // chunk, gradient_own)
-    for o, t in others:
-        pltpu.make_async_copy(pre_all.at[i], pre_all.at[t], pre_r.at[o - 1]).wait()
-    cross(2)
     cross(3)
     cross(1)
     send_cross(2)

time: 44 us -> 44 us (level)
  no operation moved by 1% of the time
where the time goes in v6:
time: 44 us; the launch traced here: 43.8 us
  Pallas kernels  43.1 us (98%)
  between operations  0.64 us (1%)
    pallas_call x1, Pallas kernels, shards(): pl.pallas_call(functools.partial(kernel, (n_dp, n_e, slot, chunk, deep)),...  41.1 us
    pallas_call x1, Pallas kernels, shards(): pl.pallas_call(functools.partial(finish, packed, ff), out_shape=tuple((ja...  1.98 us

profile of v6, /device:TPU:0, one launch (start us, length us, event | category | flops | bytes accessed | tf_op | source)
XLA Modules:
  0.0 43.8 jit_solution(10932920954220783129)
XLA Ops:
  0.6 41.1 %shard_map.93 = (bf16[2,16,8,2304]{3,2,1,0:T(8,128)(2,1)S(1)}, bf16[3,128,128]{2,1,0:T(8,128)(2,1)S(1)}, bf16[1,1040,1536]{2,1,0:T(8,128)(2,1)S(1)}, f32[1,1536]{1,0:T(1,128)S(1)}, f32[1,1040]{1,0:T(1,128)S(1)}) custom-call(bf16[1040,128]{1,0:T(8,128)(2,1)} %bitcast.5, s32[1,128]{1,0:T(1,128)} %bitcast.6, bf16[192,3072]{1,0:T(8,128)(2,1)} %pre.1, ...), custom_call_target="tpu_custom_call" | custom-call | tf_op jit(solution)/shard_map/pallas_call | solution.py:406
  41.8 2.0 %shard_map.94 = (bf16[128,3072]{1,0:T(8,128)(2,1)}, bf16[1,1040,1536]{2,1,0:T(8,128)(2,1)}, f32[1,1536]{1,0:T(1,128)}, f32[1,1040]{1,0:T(1,128)}) custom-call(bf16[2,16,8,2304]{3,2,1,0:T(8,128)(2,1)S(1)} %get-tuple-element.13.ret, bf16[3,128,128]{2,1,0:T(8,128)(2,1)S(1)} %get-tuple-element.14.place, bf16[1,1040,1536]{2,1,0:T(8,128)(2,1)S(1)} %get-tuple-element.15.neww, ...), custom_call_target="tpu_custom_call" | custom-call | tf_op jit(solution)/shard_map/pallas_call | solution.py:440

commit v7 on v6

--- a/solution.py
+++ b/solution.py
@@ -276,7 +276,7 @@
     back_cross(0)
     @pl.when(inner)
     def _():
-        send_cross(0, 0, g // 2)
+        send_cross(0, 0, 3 * g // 4)
 
 
     loads[4].wait()
@@ -312,7 +312,7 @@
 
     @pl.when(inner)
     def _():
-        send_cross(0, g // 2, g // 2)
+        send_cross(0, 3 * g // 4, g - 3 * g // 4)
 
     @pl.when(jnp.logical_not(inner))
     def _():

time: 44 us -> 44.1 us (level)
  no operation moved by 1% of the time
where the time goes in v7:
time: 44.1 us; the launch traced here: 43.8 us
  Pallas kernels  43.1 us (98%)
  between operations  0.64 us (1%)
    pallas_call x1, Pallas kernels, shards(): pl.pallas_call(functools.partial(kernel, (n_dp, n_e, slot, chunk, deep)),...  41.1 us
    pallas_call x1, Pallas kernels, shards(): pl.pallas_call(functools.partial(finish, packed, ff), out_shape=tuple((ja...  1.98 us

profile of v7, /device:TPU:0, one launch (start us, length us, event | category | flops | bytes accessed | tf_op | source)
XLA Modules:
  0.0 43.8 jit_solution(14689555001318810037)
XLA Ops:
  0.6 41.1 %shard_map.93 = (bf16[2,16,8,2304]{3,2,1,0:T(8,128)(2,1)S(1)}, bf16[3,128,128]{2,1,0:T(8,128)(2,1)S(1)}, bf16[1,1040,1536]{2,1,0:T(8,128)(2,1)S(1)}, f32[1,1536]{1,0:T(1,128)S(1)}, f32[1,1040]{1,0:T(1,128)S(1)}) custom-call(bf16[1040,128]{1,0:T(8,128)(2,1)} %bitcast.5, s32[1,128]{1,0:T(1,128)} %bitcast.6, bf16[192,3072]{1,0:T(8,128)(2,1)} %pre.1, ...), custom_call_target="tpu_custom_call" | custom-call | tf_op jit(solution)/shard_map/pallas_call | solution.py:406
  41.8 2.0 %shard_map.94 = (bf16[128,3072]{1,0:T(8,128)(2,1)}, bf16[1,1040,1536]{2,1,0:T(8,128)(2,1)}, f32[1,1536]{1,0:T(1,128)}, f32[1,1040]{1,0:T(1,128)}) custom-call(bf16[2,16,8,2304]{3,2,1,0:T(8,128)(2,1)S(1)} %get-tuple-element.13.ret, bf16[3,128,128]{2,1,0:T(8,128)(2,1)S(1)} %get-tuple-element.14.place, bf16[1,1040,1536]{2,1,0:T(8,128)(2,1)S(1)} %get-tuple-element.15.neww, ...), custom_call_target="tpu_custom_call" | custom-call | tf_op jit(solution)/shard_map/pallas_call | solution.py:440
